TPU v7x, 256 devices: a whole 4x4x8 slice. The times are simulated.
256 devices in a mesh: seq: 16 (over x_hi, z), rep: 16 (over y, x_lo, core).
Axes of the slice: x: 4 (x_hi: 2, x_lo: 2; x = x_hi * 2 + x_lo), y: 4, z: 8, core: 2. Of those that a mesh axis runs over, the one named last changes fastest.
Arguments:
- t_query: bfloat16 [16, 2048, 4096], P('rep', 'seq'), may hold values from -45 to 45
- t_key: bfloat16 [16, 2048, 512], P('rep', 'seq'), may hold values from -4 to 4
- t_value: bfloat16 [16, 2048, 512], P('rep', 'seq'), may hold values from -6 to 6
- s_query: bfloat16 [16, 2048, 2048], P('rep', 'seq'), may hold values from -45 to 45
- s_key: bfloat16 [16, 2048, 512], P('rep', 'seq'), may hold values from -4 to 4
- student_value: bfloat16 [16, 2048, 512], P('rep', 'seq'), may hold values from -6 to 6
- student_wo: bfloat16 [2048, 2048], P('seq'), may hold values from -0.125 to 0.125
- projection: bfloat16 [4096, 2048], P('seq'), may hold values from -0.09375 to 0.09375
- doc_ids: int32 [16, 2048], P('rep'), may hold values from 0 to 15, never falling along the last dimension, each value on 1 to 512 neighbouring positions
- span_order: int32 [16, 32], P('rep'), may hold values from 0 to 31, each once within a row
Outputs:
- seq_loss: float32 [16], P('rep')
- d_wo: float32 [2048, 2048], P('seq', 'rep')
- d_query: bfloat16 [16, 2048, 2048], P('rep', 'seq')
- d_key: bfloat16 [16, 2048, 512], P('rep', 'seq')
- d_value: bfloat16 [16, 2048, 512], P('rep', 'seq')
All inputs are finite; a program needn't handle non-finite values.
Results may differ from a plain program's by a relative error of at most 0.018.
The roundings to bfloat16 on the way count: a program that leaves them out, or rounds other values in their place, can miss the bound.
Values may be sent and summed in bfloat16 or wider, within the bound.
No kernel may reach another device: no remote copies, remote signals or barrier semaphores. Data moves between devices by JAX's collectives and lax.ppermute only.
A program may use at most 128 MiB of HBM per device.

v0:
```python
import math
import jax
import jax.numpy as jnp
from jax import lax
from jax.sharding import PartitionSpec as P

HEAD_WIDTH = 128
MASKED = -1e30


def stored_positions(order_row, length):
    half_len = length // order_row.shape[0]
    offsets = jnp.arange(half_len, dtype=jnp.int32)
    return (order_row[:, None] * half_len + offsets[None, :]).reshape(length)


def head_attention(queries, key_rows, val_rows, positions, stored_docs):
    length = queries.shape[0]
    row_block = math.gcd(length, 512)
    scaling = 1.0 / math.sqrt(HEAD_WIDTH)

    def one_block(block_id):
        first_row = block_id * row_block
        q_block = lax.dynamic_slice_in_dim(queries, first_row, row_block, 0)
        q_pos = lax.dynamic_slice_in_dim(positions, first_row, row_block, 0)
        q_docs = lax.dynamic_slice_in_dim(stored_docs, first_row, row_block, 0)
        allowed = (q_docs[:, None] == stored_docs[None, :]) & (positions[None, :] <= q_pos[:, None])
        scores = (
            jnp.einsum("qhd,kd->hqk", q_block, key_rows, preferred_element_type=jnp.float32)
            * scaling
        )
        scores = jnp.where(allowed, scores, MASKED)
        maximum = jnp.max(scores, axis=2, keepdims=True)
        weights = jnp.where(allowed, jnp.exp(scores - maximum), 0.0)
        totals = jnp.sum(weights, axis=2, keepdims=True)
        prob_rows = (weights / totals).astype(jnp.bfloat16)
        mixed_rows = jnp.einsum(
            "hqk,kd->qhd", prob_rows, val_rows, preferred_element_type=jnp.float32
        )
        return (prob_rows, mixed_rows.astype(jnp.bfloat16))

    block_ids = jnp.arange(length // row_block, dtype=jnp.int32)
    return lax.map(one_block, block_ids)


def shards(
    t_query,
    t_key,
    t_value,
    s_query,
    s_key,
    student_value,
    student_wo,
    projection,
    doc_ids,
    span_order,
):
    groups = lax.axis_size("seq")
    my_index = lax.axis_index("seq")
    tokens = t_query.shape[1]
    length = tokens * groups
    scaling = 1.0 / math.sqrt(HEAD_WIDTH)
    positions = stored_positions(span_order[0], length)
    stored_docs = jnp.take(doc_ids[0], positions)
    first_own = my_index * tokens
    own_pos = lax.dynamic_slice_in_dim(positions, first_own, tokens, 0)
    own_docs = lax.dynamic_slice_in_dim(stored_docs, first_own, tokens, 0)
    t_heads_all = t_query.shape[2] // HEAD_WIDTH
    t_kv = t_key.shape[2] // HEAD_WIDTH
    t_local = t_heads_all // groups
    t_share = t_heads_all // t_kv
    own_queries = t_query[0].reshape(tokens, t_kv, t_share, HEAD_WIDTH)
    start_state = (
        jnp.full((t_kv, t_share, tokens), MASKED, jnp.float32),
        jnp.zeros((t_kv, t_share, tokens), jnp.float32),
        jnp.zeros((t_kv, t_share, tokens, HEAD_WIDTH), jnp.float32),
    )
    carried = start_state
    key_piece = lax.all_gather(t_key[0], "seq", axis=0, tiled=True)
    val_piece = lax.all_gather(t_value[0], "seq", axis=0, tiled=True)
    row_count = key_piece.shape[0]
    sub_rows = math.gcd(row_count, 512)
    for offset in range(0, row_count, sub_rows):
        key_block = key_piece[offset : offset + sub_rows].reshape(sub_rows, t_kv, HEAD_WIDTH)
        val_block = val_piece[offset : offset + sub_rows].reshape(sub_rows, t_kv, HEAD_WIDTH)
        key_pos = lax.dynamic_slice_in_dim(positions, offset, sub_rows, 0)
        key_docs = lax.dynamic_slice_in_dim(stored_docs, offset, sub_rows, 0)
        allowed = (own_docs[:, None] == key_docs[None, :]) & (key_pos[None, :] <= own_pos[:, None])

        def absorb(states):
            running_max, running_sum, accumulated = states
            scores = (
                jnp.einsum(
                    "tkgd,skd->kgts", own_queries, key_block, preferred_element_type=jnp.float32
                )
                * scaling
            )
            scores = jnp.where(allowed, scores, MASKED)
            new_max = jnp.maximum(running_max, jnp.max(scores, axis=3))
            weights = jnp.where(allowed, jnp.exp(scores - new_max[..., None]), 0.0)
            factor = jnp.exp(running_max - new_max)
            running_sum = running_sum * factor + jnp.sum(weights, axis=3)
            accumulated = accumulated * factor[..., None] + jnp.einsum(
                "kgts,skd->kgtd",
                weights.astype(jnp.bfloat16),
                val_block,
                preferred_element_type=jnp.float32,
            )
            return (new_max, running_sum, accumulated)

        carried = lax.cond(jnp.any(allowed), absorb, lambda unchanged: unchanged, carried)
    running_max, running_sum, accumulated = carried
    teacher_rows = (accumulated / running_sum[..., None]).astype(jnp.bfloat16)
    teacher_rows = jnp.transpose(teacher_rows, (2, 0, 1, 3)).reshape(
        tokens, groups, t_local * HEAD_WIDTH
    )
    teacher_out = lax.all_to_all(
        teacher_rows, "seq", split_axis=1, concat_axis=0, tiled=True
    ).reshape(length, t_local * HEAD_WIDTH)
    s_heads_all = s_query.shape[2] // HEAD_WIDTH
    s_local = s_heads_all // groups
    s_kv = s_key.shape[2] // HEAD_WIDTH
    student_rows = s_query[0].reshape(tokens, groups, s_local * HEAD_WIDTH)
    student_heads = lax.all_to_all(student_rows, "seq", split_axis=1, concat_axis=0, tiled=True)
    all_keys, all_values = (
        lax.all_gather(s_key[0], "seq", axis=0, tiled=True),
        lax.all_gather(student_value[0], "seq", axis=0, tiled=True),
    )
    kv_index = my_index // (groups // s_kv)
    key_heads = lax.dynamic_slice_in_dim(all_keys, kv_index * HEAD_WIDTH, HEAD_WIDTH, 1)
    val_heads = lax.dynamic_slice_in_dim(all_values, kv_index * HEAD_WIDTH, HEAD_WIDTH, 1)
    prob_blocks, student_blocks = head_attention(
        student_heads, key_heads, val_heads, positions, stored_docs
    )
    student_out = student_blocks.reshape(length, s_local * HEAD_WIDTH)
    width_all = student_wo.shape[1]
    own_diff = lax.psum_scatter(
        (
            jnp.dot(student_out, student_wo, preferred_element_type=jnp.float32)
            - jnp.dot(teacher_out, projection, preferred_element_type=jnp.float32)
        ).astype(jnp.bfloat16),
        "seq",
        scatter_dimension=0,
        tiled=True,
    ).astype(jnp.float32)
    squares = lax.psum(jnp.sum(own_diff * own_diff), "seq")
    seq_loss = (squares / (length * width_all)).reshape(1)
    own_grad = own_diff.astype(jnp.bfloat16)
    piece_rows = lax.all_gather(own_grad, "seq", axis=0, tiled=True)
    attn_rows = jnp.einsum("rc,hc->rh", piece_rows, student_wo, preferred_element_type=jnp.float32)
    d_attn = attn_rows
    d_weight = jnp.einsum("rh,rc->hc", student_out, piece_rows, preferred_element_type=jnp.float32)
    d_attn, d_weight = (d_attn, d_weight)
    row_block = math.gcd(length, 512)
    blocks = length // row_block
    grad_blocks = d_attn.astype(jnp.bfloat16).reshape(blocks, row_block, s_local, HEAD_WIDTH)
    query_blocks = student_heads.reshape(blocks, row_block, s_local, HEAD_WIDTH)

    def back_block(carried, inputs):
        d_key, d_value = carried
        prob_block, out_block, grad_block, query_block = inputs
        row_delta = jnp.sum(grad_block.astype(jnp.float32) * out_block.astype(jnp.float32), axis=2)
        d_value = d_value + jnp.einsum(
            "hqk,qhd->kd", prob_block, grad_block, preferred_element_type=jnp.float32
        )
        d_prob = jnp.einsum(
            "qhd,kd->hqk", grad_block, val_heads, preferred_element_type=jnp.float32
        )
        d_score = (
            prob_block.astype(jnp.float32) * (d_prob - jnp.transpose(row_delta)[:, :, None])
        ).astype(jnp.bfloat16)
        d_query = (
            jnp.einsum("hqk,kd->qhd", d_score, key_heads, preferred_element_type=jnp.float32)
            * scaling
        ).astype(jnp.bfloat16)
        d_key = d_key + jnp.einsum(
            "hqk,qhd->kd", d_score, query_block, preferred_element_type=jnp.float32
        )
        return ((d_key, d_value), d_query)

    zero_rows = jnp.zeros((length, HEAD_WIDTH), jnp.float32)
    (d_key, d_value), d_query = lax.scan(
        back_block, (zero_rows, zero_rows), (prob_blocks, student_blocks, grad_blocks, query_blocks)
    )
    query_part = d_query.reshape(length, 1, s_local * HEAD_WIDTH)
    key_part = (d_key * scaling).astype(jnp.bfloat16).reshape(length, 1, HEAD_WIDTH)
    value_part = d_value.astype(jnp.bfloat16).reshape(length, 1, HEAD_WIDTH)
    back_query, back_key, back_value = (
        lax.all_to_all(query_part, "seq", split_axis=0, concat_axis=1, tiled=True),
        lax.all_to_all(key_part, "seq", split_axis=0, concat_axis=1, tiled=True),
        lax.all_to_all(value_part, "seq", split_axis=0, concat_axis=1, tiled=True),
    )
    repeat_count = groups // s_kv

    def merge_slots(slot_rows):
        summed = (
            slot_rows.reshape(tokens, s_kv, repeat_count, HEAD_WIDTH)
            .astype(jnp.float32)
            .sum(axis=2)
        )
        return summed.astype(jnp.bfloat16).reshape(1, tokens, s_kv * HEAD_WIDTH)

    weight_share = lax.psum_scatter(
        d_weight.astype(jnp.bfloat16), "rep", scatter_dimension=1, tiled=True
    ).astype(jnp.float32)
    return (
        seq_loss,
        weight_share,
        back_query.reshape(1, tokens, s_heads_all * HEAD_WIDTH),
        merge_slots(back_key),
        merge_slots(back_value),
    )


def solution(mesh):
    in_specs = (
        P("rep", "seq", None),
        P("rep", "seq", None),
        P("rep", "seq", None),
        P("rep", "seq", None),
        P("rep", "seq", None),
        P("rep", "seq", None),
        P("seq", None),
        P("seq", None),
        P("rep", None),
        P("rep", None),
    )
    out_specs = (
        P("rep"),
        P("seq", "rep"),
        P("rep", "seq", None),
        P("rep", "seq", None),
        P("rep", "seq", None),
    )
    return jax.shard_map(shards, mesh=mesh, in_specs=in_specs, out_specs=out_specs, check_vma=False)
```

profile of v0, /device:TPU:4, one launch (start us, length us, event | category | flops | bytes accessed | tf_op | source)
XLA Modules:
  0.0 964.9 jit_solution(540645325133309990)
XLA Ops:
  14.1 11.4 %all-to-all-start = ((bf16[128,16,128]{0,2,1:T(8,128)(2,1)}), bf16[128,16,128]{0,2,1:T(8,128)(2,1)S(1)}, u32[]{:S(2)}, u32[]{:S(2)}) async-start(bf16[128,16,128]{0,2,1:T(8,128)(2,1)} %bitcast.19), calls=%async_computation | async-start | bytes 1048576 | tf_op jit(solution)/shard_map/all_to_all | solution.py:124
  26.5 11.8 %gather_fusion = s32[2048]{0:T(1024)S(1)} fusion(s32[2048]{0:T(1024)S(1)} %bitcast.316, s32[2048]{0:T(1024)S(1)} %broadcast_clamp_fusion), kind=kCustom, calls=%fused_computation | custom fusion | bytes 24576 | tf_op jit(solution)/shard_map/jit(_take)/gather | solution.py:64
  45.3 55.4 %all-gather.16.cloned.1.call-done = bf16[1,2048,512]{1,2,0:T(8,128)(2,1)} async-done(((bf16[1,128,512]{1,2,0:T(8,128)(2,1)}), bf16[1,2048,512]{1,2,0:T(8,128)(2,1)}) %all-gather.16.cloned.1.call-update) | async-done | bytes 2097168 | tf_op jit(solution)/shard_map/all_gather | solution.py:79
  101.9 83.1 %all-gather.18.cloned.1.call-done = bf16[1,2048,512]{1,2,0:T(8,128)(2,1)} async-done(((bf16[1,128,512]{1,2,0:T(8,128)(2,1)}), bf16[1,2048,512]{1,2,0:T(8,128)(2,1)}) %all-gather.18.cloned.1.call-update) | async-done | bytes 2097168 | tf_op jit(solution)/shard_map/all_gather | solution.py:80
  187.1 10.2 %conditional.4 = (f32[4,8,128]{2,1,0:T(8,128)}, f32[4,8,128]{2,1,0:T(8,128)S(1)}, f32[4,8,128,128]{3,2,1,0:T(8,128)}) conditional(s32[]{:T(128)} %convert_element_type.124, () %tuple.44, (pred[128,512]{0,1:T(8,128)(4,1)S(1)}, bf16[512,4,128]{0,2,1:T(8,128)(2,1)S(1)}, bf16[128,4,8,128]{0,3,2,1:T(8,128)(2,1)S(1)}, ...), branch_computations={%region_8.9_spmd, %region_9.0_spmd} | conditional | flops 1101545472 | bytes 29736984 | solution.py:111
  189.2 4.6 fusion.8
  197.3 11.0 %conditional.5 = ((f32[4,8,128]{2,1,0:T(8,128)}, f32[4,8,128]{2,1,0:T(8,128)S(1)}, f32[4,8,128,128]{3,2,1,0:T(8,128)})) conditional(s32[]{:T(128)} %convert_element_type.123, (f32[4,8,128]{2,1,0:T(8,128)}, f32[4,8,128]{2,1,0:T(8,128)S(1)}, f32[4,8,128,128]{3,2,1,0:T(8,128)}) %conditional.4, (pred[128,512]{0,1:T(8,128)(4,1)S(1)}, ...), branch_computations={%region_12.13_spmd, %region_13.16_spmd} | conditional | flops 1102061568 | bytes 34013244 | solution.py:111
  202.4 5.3 multiply_add_fusion
  208.3 13.6 %conditional.6 = ((f32[4,8,128]{2,1,0:T(8,128)}, f32[4,8,128]{2,1,0:T(8,128)S(1)}, f32[4,8,128,128]{3,2,1,0:T(8,128)})) conditional(s32[]{:T(128)} %convert_element_type.122, (f32[4,8,128]{2,1,0:T(8,128)}, f32[4,8,128]{2,1,0:T(8,128)S(1)}, f32[4,8,128,128]{3,2,1,0:T(8,128)}) %get-tuple-element.785, (pred[128,512]{0,1:T(8,128)(4,1)S(1)}, ...), branch_computations={%region_16.17_spmd, %region_17.20_spmd} | conditional | flops 1102061568 | bytes 34013216 | solution.py:111
  216.0 5.3 multiply_add_fusion.2
  221.8 14.4 %conditional.7 = (f32[4,8,128]{2,1,0:T(8,128)S(1)}, f32[4,8,128,128]{2,3,1,0:T(8,128)S(1)}) conditional(s32[]{:T(128)} %convert_element_type.121, (f32[4,8,128]{2,1,0:T(8,128)S(1)}, f32[4,8,128,128]{3,2,1,0:T(8,128)}) %tuple.48, (pred[128,512]{0,1:T(8,128)(4,1)S(1)}, bf16[2048,512]{0,1:T(8,128)(2,1)}, bf16[128,4,8,128]{0,3,2,1:T(8,128)(2,1)S(1)}, ...), branch_computations={%region_20.21_spmd, %region_21.24_spmd} | conditional | flops 1102061568 | bytes 38174736 | solution.py:111
  229.1 5.3 multiply_add_fusion.4
  237.6 7.3 all-to-all-start.1
  245.0 35.6 %all-gather.14.cloned.1.call-done = bf16[1,2048,512]{2,1,0:T(8,128)(2,1)} async-done(((bf16[1,128,512]{2,1,0:T(8,128)(2,1)}), bf16[1,2048,512]{2,1,0:T(8,128)(2,1)}) %all-gather.14.cloned.1.call-update) | async-done | bytes 2097168 | tf_op jit(solution)/shard_map/all_gather | solution.py:127
  282.6 82.9 %all-gather.12.cloned.1.call-done = bf16[1,2048,512]{2,1,0:T(8,128)(2,1)} async-done(((bf16[1,128,512]{2,1,0:T(8,128)(2,1)}), bf16[1,2048,512]{2,1,0:T(8,128)(2,1)}) %all-gather.12.cloned.1.call-update) | async-done | bytes 2097168 | tf_op jit(solution)/shard_map/all_gather | solution.py:126
  368.2 48.5 %while.28 = (s32[]{:T(128)}, bf16[4,1,512,2048]{3,2,1,0:T(8,128)(2,1)}, bf16[4,512,1,128]{3,1,2,0:T(8,128)(2,1)}, s32[4]{0:T(128)S(1)}, s32[2048]{0:T(1024)S(1)}...) while((s32[]{:T(128)}, ...), condition=%wide.region_3.4_spmd.clone, body=%wide.region_0.3_spmd.clone.sunk | while | flops 570491904 | bytes 20315468 | solution.py:43
  416.7 9.1 fusion.98
  426.3 11.3 %subtract_convert_fusion = bf16[2048,2048]{1,0:T(8,128)(2,1)} fusion(f32[2048,2048]{1,0:T(8,128)} %fusion.98, bf16[2048,256]{1,0:T(8,128)(2,1)S(1)} %bitcast.323, bf16[256,2048]{1,0:T(8,128)(2,1)S(1)} %copy-done), kind=kOutput, calls=%fused_computation.101 | convolution fusion | flops 2155872256 | bytes 27262976 | tf_op jit(solution)/shard_map/dot_general | solution.py:140
  437.9 221.5 %reduce-scatter.5.cloned.1.call-done = bf16[128,2048]{1,0:T(8,128)(2,1)} async-done(((bf16[2048,2048]{1,0:T(8,128)(2,1)}), bf16[128,2048]{1,0:T(8,128)(2,1)}) %reduce-scatter.5.cloned.1.call-update) | async-done | bytes 524304 | tf_op jit(solution)/shard_map/reduce_scatter | solution.py:137
  659.5 135.7 %all-gather.10.cloned.1.call-done = bf16[2048,2048]{1,0:T(8,128)(2,1)} async-done(((bf16[128,2048]{1,0:T(8,128)(2,1)}), bf16[2048,2048]{1,0:T(8,128)(2,1)}) %all-gather.10.cloned.1.call-update) | async-done | bytes 8388624 | tf_op jit(solution)/shard_map/all_gather | solution.py:149
  795.2 6.5 convolution_convert_fusion
  802.6 46.5 %while.29 = (s32[]{:T(128)}, f32[2048,128]{1,0:T(8,128)}, f32[2048,128]{1,0:T(8,128)}, bf16[4,512,1,128]{3,1,2,0:T(8,128)(2,1)}, bf16[4,1,512,2048]{3,2,1,0:T(8,...) while((s32[]{:T(128)}, f32[2048,128]{1,0:T(8,128)}, ...), condition=%wide.region_30.31_spmd.clone, body=%wide.region_28.30_spmd.clone.sunk | while | flops 1079377408 | bytes 18619552 | solution.py:182
  821.9 3.6 convolution_add_fusion.5
  833.7 3.6 convolution_add_fusion.5
  845.5 3.6 convolution_add_fusion.5
  853.4 7.3 all-to-all-start.4
  862.7 11.7 %all-to-all-done.4 = bf16[16,2,8192]{2,1,0:T(2,128)(2,1)S(1)} async-done(((bf16[16,2,8192]{2,1,0:T(2,128)(2,1)}), bf16[16,2,8192]{2,1,0:T(2,128)(2,1)S(1)}, u32[]{:S(2)}, u32[]{:S(2)}) %all-to-all-start.4) | async-done | bytes 524320 | tf_op jit(solution)/shard_map/all_to_all | solution.py:191
  874.4 7.4 all-to-all-start.3
  881.8 4.8 convolution_convert_fusion.1
  890.7 4.4 all-to-all-done.3
  895.1 7.2 all-to-all-start.2
  903.1 43.3 %psum.7 = f32[]{:T(128)} all-reduce(f32[]{:T(128)} %multiply_reduce_fusion.1), channel_id=1, replica_groups=mesh['seq'=16,'rep'=16] {'seq'}, use_global_device_ids=true, to_apply=%region_26.27 | all-reduce | flops 1 | bytes 8 | tf_op jit(solution)/shard_map/psum | solution.py:146
  (173 shorter events, 153.7 us)
Async XLA Ops:
  7.2 419.1 %copy-start = (bf16[256,2048]{1,0:T(8,128)(2,1)S(1)}, bf16[256,2048]{1,0:T(8,128)(2,1)}, u32[]{:S(2)}) copy-start(bf16[256,2048]{1,0:T(8,128)(2,1)} %param.29) | copy-start | bytes 3145732
  7.2 19.3 %copy-start.1 = (s32[1,2048]{1,0:T(1,128)S(1)}, s32[1,2048]{1,0:T(1,128)}, u32[]{:S(2)}) copy-start(s32[1,2048]{1,0:T(1,128)} %param.30) | copy-start | bytes 24580
  7.2 93.5 %all-gather.16.cloned.1.call-start = ((), (), s32[]{:S(2)}) async-start(), calls=%async_computation.11 | async-start | bytes 2228224 | tf_op jit(solution)/shard_map/all_gather | solution.py:79
  9.0 176.1 %all-gather.18.cloned.1.call-start = ((), (), s32[]{:S(2)}) async-start(), calls=%async_computation.12 | async-start | bytes 2228224 | tf_op jit(solution)/shard_map/all_gather | solution.py:80
  10.7 269.9 %all-gather.14.cloned.1.call-start = ((), (), s32[]{:S(2)}) async-start(), calls=%async_computation.10 | async-start | bytes 2228224 | tf_op jit(solution)/shard_map/all_gather | solution.py:127
  11.5 354.0 %all-gather.12.cloned.1.call-start = ((), (), s32[]{:S(2)}) async-start(), calls=%async_computation.9 | async-start | bytes 2228224 | tf_op jit(solution)/shard_map/all_gather | solution.py:126
  14.1 30.2 %all-to-all-start = ((bf16[128,16,128]{0,2,1:T(8,128)(2,1)}), bf16[128,16,128]{0,2,1:T(8,128)(2,1)S(1)}, u32[]{:S(2)}, u32[]{:S(2)}) async-start(bf16[128,16,128]{0,2,1:T(8,128)(2,1)} %bitcast.19), calls=%async_computation | async-start | bytes 1048576 | tf_op jit(solution)/shard_map/all_to_all | solution.py:124
  199.5 2.9 copy-start.6
  237.6 188.2 %all-to-all-start.1 = ((bf16[128,16,256]{0,2,1:T(8,128)(2,1)}), bf16[128,16,256]{0,2,1:T(8,128)(2,1)S(1)}, u32[]{:S(2)}, u32[]{:S(2)}) async-start(bf16[128,16,256]{0,2,1:T(8,128)(2,1)} %bitcast.321), calls=%async_computation.1 | async-start | bytes 2097152 | tf_op jit(solution)/shard_map/all_to_all | solution.py:117
  244.8 414.6 %reduce-scatter.5.cloned.1.call-start = ((), (), s32[]{:S(2)}) async-start(), calls=%async_computation.7 | async-start | bytes 8912896 | tf_op jit(solution)/shard_map/reduce_scatter | solution.py:137
  368.2 48.5 %copy-start.3 = (bf16[128,2048]{1,0:T(8,128)(2,1)S(1)}, bf16[128,2048]{1,0:T(8,128)(2,1)}, u32[]{:S(2)}) copy-start(bf16[128,2048]{1,0:T(8,128)(2,1)} %param.28) | copy-start | bytes 1572868
  437.6 357.6 %copy-start.4 = (bf16[128,2048]{1,0:T(8,128)(2,1)S(1)}, bf16[128,2048]{1,0:T(8,128)(2,1)}, u32[]{:S(2)}) copy-start(bf16[128,2048]{1,0:T(8,128)(2,1)} %param.28) | copy-start | bytes 1572868
  437.7 357.6 %all-gather.10.cloned.1.call-start = ((), (), s32[]{:S(2)}) async-start(), calls=%async_computation.8 | async-start | bytes 8912896 | tf_op jit(solution)/shard_map/all_gather | solution.py:149
  806.3 2.8 copy-start.5
  817.4 3.2 copy-start.5
  829.2 3.2 copy-start.5
  841.0 3.2 copy-start.5
  853.4 21.0 %all-to-all-start.4 = ((bf16[16,2,8192]{2,1,0:T(2,128)(2,1)}), bf16[16,2,8192]{2,1,0:T(2,128)(2,1)S(1)}, u32[]{:S(2)}, u32[]{:S(2)}) async-start(bf16[16,2,8192]{2,1,0:T(2,128)(2,1)} %reshape.415), calls=%async_computation.5 | async-start | bytes 1048576 | tf_op jit(solution)/shard_map/all_to_all | solution.py:191
  874.4 20.7 %all-to-all-start.3 = ((bf16[16,2,8192]{2,1,0:T(2,128)(2,1)}), bf16[16,2,8192]{2,1,0:T(2,128)(2,1)S(1)}, u32[]{:S(2)}, u32[]{:S(2)}) async-start(bf16[16,2,8192]{2,1,0:T(2,128)(2,1)} %reshape.413), calls=%async_computation.4 | async-start | bytes 1048576 | tf_op jit(solution)/shard_map/all_to_all | solution.py:190
  881.8 73.4 %reduce-scatter.7.cloned.1.call-start = ((), (), s32[]{:S(2)}) async-start(), calls=%async_computation.13 | async-start | bytes 557056
  886.7 15.6 %copy-start.2 = (bf16[128,2048]{1,0:T(8,128)(2,1)S(1)}, bf16[128,2048]{1,0:T(8,128)(2,1)}, u32[]{:S(2)}) copy-start(bf16[128,2048]{1,0:T(8,128)(2,1)} %reduce-scatter.5.cloned.1.call-done) | copy-start | bytes 1572868
  895.1 55.2 %all-to-all-start.2 = ((bf16[16,2,8192]{2,1,0:T(2,128)(2,1)}), bf16[16,2,8192]{2,1,0:T(2,128)(2,1)}, u32[]{:S(2)}, u32[]{:S(2)}) async-start(bf16[16,2,8192]{2,1,0:T(2,128)(2,1)} %reshape.411), calls=%async_computation.3 | async-start | bytes 1048576 | tf_op jit(solution)/shard_map/all_to_all | solution.py:189
Sparse Core Ops, SparseCore 0:
  11.0 89.5 all-gather.15
  103.7 81.3 all-gather.17
  187.7 92.9 all-gather.13
  283.1 82.2 all-gather.11
  437.8 221.6 reduce-scatter.4
  661.9 133.2 all-gather.9
  887.8 67.2 reduce-scatter.6
where the time goes:
time: 975 us; the launch traced here: 965 us
  waiting for transfers between devices  633 us (65%)
  matrix products  124 us (13%)
  local copies, waits for them, and re-layouts  52.3 us (5%)
  other arithmetic  49 us (5%)
  blocking collectives  43.3 us (4%)
  starting transfers between devices  41.3 us (4%)
  between operations  18.9 us (2%)
    reduce_scatter x1, waiting for transfers between devices, shards(): lax.psum_scatter((jnp.dot(student_out, student_wo, preferred_element_type...  222 us
    all_gather x1, waiting for transfers between devices, shards(): piece_rows = lax.all_gather(own_grad, 'seq', axis=0, tiled=True)  136 us
    all_gather x1, waiting for transfers between devices, shards(): val_piece = lax.all_gather(t_value[0], 'seq', axis=0, tiled=True)  83.1 us
    all_gather x1, waiting for transfers between devices, shards(): lax.all_gather(s_key[0], 'seq', axis=0, tiled=True)  82.9 us
    all_gather x1, waiting for transfers between devices, shards(): key_piece = lax.all_gather(t_key[0], 'seq', axis=0, tiled=True)  55.4 us
    psum x1, blocking collectives, shards(): squares = lax.psum(jnp.sum(own_diff * own_diff), 'seq')  43.3 us
    all_gather x1, waiting for transfers between devices, shards(): lax.all_gather(student_value[0], 'seq', axis=0, tiled=True)  35.6 us
    dot_general x4, matrix products, absorb(): jnp.einsum('kgts,skd->kgtd', weights.astype(jnp.bfloat16), val_block, pre...  20.4 us
  transfers between devices with their start and end apart: 12, of which 9 were waited for; matrix products, arithmetic and copies ran while one was open for 16% of the time, Pallas kernels for 0%

commit v1 on v0

--- a/solution.py
+++ b/solution.py
@@ -146,7 +146,9 @@
     squares = lax.psum(jnp.sum(own_diff * own_diff), "seq")
     seq_loss = (squares / (length * width_all)).reshape(1)
     own_grad = own_diff.astype(jnp.bfloat16)
-    piece_rows = lax.all_gather(own_grad, "seq", axis=0, tiled=True)
+    piece_rows = jnp.concatenate(
+        lax.all_to_all(jnp.stack([own_grad] * lax.axis_size("seq")), "seq", 0, 0), axis=0
+    )
     attn_rows = jnp.einsum("rc,hc->rh", piece_rows, student_wo, preferred_element_type=jnp.float32)
     d_attn = attn_rows
     d_weight = jnp.einsum("rh,rc->hc", student_out, piece_rows, preferred_element_type=jnp.float32)

time: 975 us -> 1040 us (1.067)
  waiting for transfers between devices: 633 us -> 676 us
  starting transfers between devices: 41.3 us -> 56.8 us
    all_to_all x0 -> x1, waiting for transfers between devices: none -> 179 us  [shards(): lax.all_to_all(jnp.stack([own_grad] * lax.axis_size('seq')), 'seq', 0, 0)]
    all_gather x1 -> x0, waiting for transfers between devices: 136 us -> none  [shards(): piece_rows = lax.all_gather(own_grad, 'seq', axis=0, tiled=True)]
  transfers between devices with their start and end apart: 12 -> 12, of which waited for: 9 -> 9; matrix products, arithmetic and copies ran while one was open for 16% -> 15% of each run, Pallas kernels for 0% -> 0%
where the time goes in v1:
time: 1040 us; the launch traced here: 1030 us
  waiting for transfers between devices  676 us (65%)
  matrix products  124 us (12%)
  local copies, waits for them, and re-layouts  57.6 us (6%)
  starting transfers between devices  56.8 us (5%)
  other arithmetic  49 us (5%)
  blocking collectives  43.3 us (4%)
  between operations  18.9 us (2%)
    reduce_scatter x1, waiting for transfers between devices, shards(): lax.psum_scatter((jnp.dot(student_out, student_wo, preferred_element_type...  222 us
    all_to_all x1, waiting for transfers between devices, shards(): lax.all_to_all(jnp.stack([own_grad] * lax.axis_size('seq')), 'seq', 0, 0)  179 us
    all_gather x1, waiting for transfers between devices, shards(): val_piece = lax.all_gather(t_value[0], 'seq', axis=0, tiled=True)  83.1 us
    all_gather x1, waiting for transfers between devices, shards(): lax.all_gather(s_key[0], 'seq', axis=0, tiled=True)  82.9 us
    all_gather x1, waiting for transfers between devices, shards(): key_piece = lax.all_gather(t_key[0], 'seq', axis=0, tiled=True)  55.4 us
    psum x1, blocking collectives, shards(): squares = lax.psum(jnp.sum(own_diff * own_diff), 'seq')  43.3 us
    all_gather x1, waiting for transfers between devices, shards(): lax.all_gather(student_value[0], 'seq', axis=0, tiled=True)  35.6 us
  transfers between devices with their start and end apart: 12, of which 9 were waited for; matrix products, arithmetic and copies ran while one was open for 15% of the time, Pallas kernels for 0%

profile of v1, /device:TPU:4, one launch (start us, length us, event | category | flops | bytes accessed | tf_op | source)
XLA Modules:
  0.0 1029.0 jit_solution(13041745403591065549)
XLA Ops:
  14.1 11.4 %all-to-all-start = ((bf16[128,16,128]{0,2,1:T(8,128)(2,1)}), bf16[128,16,128]{0,2,1:T(8,128)(2,1)S(1)}, u32[]{:S(2)}, u32[]{:S(2)}) async-start(bf16[128,16,128]{0,2,1:T(8,128)(2,1)} %bitcast.19), calls=%async_computation | async-start | bytes 1048576 | tf_op jit(solution)/shard_map/all_to_all | solution.py:124
  26.5 11.8 %gather_fusion = s32[2048]{0:T(1024)S(1)} fusion(s32[2048]{0:T(1024)S(1)} %bitcast.317, s32[2048]{0:T(1024)S(1)} %broadcast_clamp_fusion), kind=kCustom, calls=%fused_computation | custom fusion | bytes 24576 | tf_op jit(solution)/shard_map/jit(_take)/gather | solution.py:64
  45.3 55.4 %all-gather.13.cloned.1.call-done = bf16[1,2048,512]{1,2,0:T(8,128)(2,1)} async-done(((bf16[1,128,512]{1,2,0:T(8,128)(2,1)}), bf16[1,2048,512]{1,2,0:T(8,128)(2,1)}) %all-gather.13.cloned.1.call-update) | async-done | bytes 2097168 | tf_op jit(solution)/shard_map/all_gather | solution.py:79
  101.9 83.1 %all-gather.15.cloned.1.call-done = bf16[1,2048,512]{1,2,0:T(8,128)(2,1)} async-done(((bf16[1,128,512]{1,2,0:T(8,128)(2,1)}), bf16[1,2048,512]{1,2,0:T(8,128)(2,1)}) %all-gather.15.cloned.1.call-update) | async-done | bytes 2097168 | tf_op jit(solution)/shard_map/all_gather | solution.py:80
  187.1 10.2 conditional.4
  189.2 4.6 fusion.8
  197.3 11.0 %conditional.5 = ((f32[4,8,128]{2,1,0:T(8,128)}, f32[4,8,128]{2,1,0:T(8,128)S(1)}, f32[4,8,128,128]{3,2,1,0:T(8,128)})) conditional(s32[]{:T(128)} %convert_element_type.123, (f32[4,8,128]{2,1,0:T(8,128)}, f32[4,8,128]{2,1,0:T(8,128)S(1)}, f32[4,8,128,128]{3,2,1,0:T(8,128)}) %conditional.4, (pred[128,512]{0,1:T(8,128)(4,1)S(1)}, ...), branch_computations={%region_12.13_spmd, %region_13.16_spmd} | conditional | flops 1102061568 | bytes 34013244 | solution.py:111
  202.4 5.3 multiply_add_fusion
  208.3 13.6 %conditional.6 = ((f32[4,8,128]{2,1,0:T(8,128)}, f32[4,8,128]{2,1,0:T(8,128)S(1)}, f32[4,8,128,128]{3,2,1,0:T(8,128)})) conditional(s32[]{:T(128)} %convert_element_type.122, (f32[4,8,128]{2,1,0:T(8,128)}, f32[4,8,128]{2,1,0:T(8,128)S(1)}, f32[4,8,128,128]{3,2,1,0:T(8,128)}) %get-tuple-element.785, (pred[128,512]{0,1:T(8,128)(4,1)S(1)}, ...), branch_computations={%region_16.17_spmd, %region_17.20_spmd} | conditional | flops 1102061568 | bytes 34013216 | solution.py:111
  216.0 5.3 multiply_add_fusion.2
  221.8 14.4 %conditional.7 = (f32[4,8,128]{2,1,0:T(8,128)S(1)}, f32[4,8,128,128]{2,3,1,0:T(8,128)S(1)}) conditional(s32[]{:T(128)} %convert_element_type.121, (f32[4,8,128]{2,1,0:T(8,128)S(1)}, f32[4,8,128,128]{3,2,1,0:T(8,128)}) %tuple.48, (pred[128,512]{0,1:T(8,128)(4,1)S(1)}, bf16[2048,512]{0,1:T(8,128)(2,1)}, bf16[128,4,8,128]{0,3,2,1:T(8,128)(2,1)S(1)}, ...), branch_computations={%region_20.21_spmd, %region_21.24_spmd} | conditional | flops 1102061568 | bytes 38174736 | solution.py:111
  229.1 5.3 multiply_add_fusion.4
  237.6 7.3 all-to-all-start.1
  245.0 35.6 %all-gather.11.cloned.1.call-done = bf16[1,2048,512]{2,1,0:T(8,128)(2,1)} async-done(((bf16[1,128,512]{2,1,0:T(8,128)(2,1)}), bf16[1,2048,512]{2,1,0:T(8,128)(2,1)}) %all-gather.11.cloned.1.call-update) | async-done | bytes 2097168 | tf_op jit(solution)/shard_map/all_gather | solution.py:127
  282.6 82.9 %all-gather.9.cloned.1.call-done = bf16[1,2048,512]{2,1,0:T(8,128)(2,1)} async-done(((bf16[1,128,512]{2,1,0:T(8,128)(2,1)}), bf16[1,2048,512]{2,1,0:T(8,128)(2,1)}) %all-gather.9.cloned.1.call-update) | async-done | bytes 2097168 | tf_op jit(solution)/shard_map/all_gather | solution.py:126
  368.2 48.5 %while.28 = (s32[]{:T(128)}, bf16[4,1,512,2048]{3,2,1,0:T(8,128)(2,1)}, bf16[4,512,1,128]{3,1,2,0:T(8,128)(2,1)}, s32[4]{0:T(128)S(1)}, s32[2048]{0:T(1024)S(1)}...) while((s32[]{:T(128)}, ...), condition=%wide.region_3.4_spmd.clone, body=%wide.region_0.3_spmd.clone.sunk | while | flops 570491904 | bytes 20315468 | solution.py:43
  416.7 9.1 fusion.98
  426.3 11.3 %subtract_convert_fusion = bf16[2048,2048]{1,0:T(8,128)(2,1)} fusion(f32[2048,2048]{1,0:T(8,128)} %fusion.98, bf16[2048,256]{1,0:T(8,128)(2,1)S(1)} %bitcast.324, bf16[256,2048]{1,0:T(8,128)(2,1)S(1)} %copy-done), kind=kOutput, calls=%fused_computation.101 | convolution fusion | flops 2155872256 | bytes 27262976 | tf_op jit(solution)/shard_map/dot_general | solution.py:140
  437.7 222.0 %reduce-scatter.5.cloned.1.call-done = bf16[128,2048]{1,0:T(8,128)(2,1)} async-done(((bf16[2048,2048]{1,0:T(8,128)(2,1)}), bf16[128,2048]{1,0:T(8,128)(2,1)}) %reduce-scatter.5.cloned.1.call-update) | async-done | bytes 524304 | tf_op jit(solution)/shard_map/reduce_scatter | solution.py:137
  659.6 5.3 stack.2
  664.9 9.3 all-to-all-start.2
  674.3 178.8 %all-to-all-done.2 = bf16[16,128,2048]{2,1,0:T(8,128)(2,1)} async-done(((bf16[16,128,2048]{2,1,0:T(8,128)(2,1)}), bf16[16,128,2048]{2,1,0:T(8,128)(2,1)}, u32[]{:S(2)}, u32[]{:S(2)}) %all-to-all-start.2) | async-done | bytes 8388640 | tf_op jit(solution)/shard_map/all_to_all | solution.py:150
  853.1 6.6 convolution_convert_fusion
  860.6 46.5 %while.29 = (s32[]{:T(128)}, f32[2048,128]{1,0:T(8,128)}, f32[2048,128]{1,0:T(8,128)}, bf16[4,512,1,128]{3,1,2,0:T(8,128)(2,1)}, bf16[4,1,512,2048]{3,2,1,0:T(8,...) while((s32[]{:T(128)}, f32[2048,128]{1,0:T(8,128)}, ...), condition=%wide.region_30.31_spmd.clone, body=%wide.region_28.30_spmd.clone.sunk | while | flops 1079377408 | bytes 18619552 | solution.py:184
  903.4 3.6 convolution_add_fusion.5
  911.3 13.7 %all-to-all-start.5 = ((bf16[16,2,8192]{2,1,0:T(2,128)(2,1)}), bf16[16,2,8192]{2,1,0:T(2,128)(2,1)S(1)}, u32[]{:S(2)}, u32[]{:S(2)}) async-start(bf16[16,2,8192]{2,1,0:T(2,128)(2,1)} %reshape.421), calls=%async_computation.6 | async-start | bytes 1048576 | tf_op jit(solution)/shard_map/all_to_all | solution.py:193
  926.9 11.5 %all-to-all-done.5 = bf16[16,2,8192]{2,1,0:T(2,128)(2,1)S(1)} async-done(((bf16[16,2,8192]{2,1,0:T(2,128)(2,1)}), bf16[16,2,8192]{2,1,0:T(2,128)(2,1)S(1)}, u32[]{:S(2)}, u32[]{:S(2)}) %all-to-all-start.5) | async-done | bytes 524320 | tf_op jit(solution)/shard_map/all_to_all | solution.py:193
  938.3 7.4 all-to-all-start.4
  945.8 4.9 convolution_convert_fusion.1
  954.7 4.4 all-to-all-done.4
  959.1 7.3 all-to-all-start.3
  967.2 43.3 %psum.7 = f32[]{:T(128)} all-reduce(f32[]{:T(128)} %multiply_reduce_fusion.1), channel_id=1, replica_groups=mesh['seq'=16,'rep'=16] {'seq'}, use_global_device_ids=true, to_apply=%region_26.27 | all-reduce | flops 1 | bytes 8 | tf_op jit(solution)/shard_map/psum | solution.py:146
  (173 shorter events, 160.6 us)
Async XLA Ops:
  7.2 419.1 %copy-start = (bf16[256,2048]{1,0:T(8,128)(2,1)S(1)}, bf16[256,2048]{1,0:T(8,128)(2,1)}, u32[]{:S(2)}) copy-start(bf16[256,2048]{1,0:T(8,128)(2,1)} %param.29) | copy-start | bytes 3145732
  7.2 19.3 %copy-start.1 = (s32[1,2048]{1,0:T(1,128)S(1)}, s32[1,2048]{1,0:T(1,128)}, u32[]{:S(2)}) copy-start(s32[1,2048]{1,0:T(1,128)} %param.30) | copy-start | bytes 24580
  7.2 93.5 %all-gather.13.cloned.1.call-start = ((), (), s32[]{:S(2)}) async-start(), calls=%async_computation.11 | async-start | bytes 2228224 | tf_op jit(solution)/shard_map/all_gather | solution.py:79
  9.0 176.1 %all-gather.15.cloned.1.call-start = ((), (), s32[]{:S(2)}) async-start(), calls=%async_computation.12 | async-start | bytes 2228224 | tf_op jit(solution)/shard_map/all_gather | solution.py:80
  10.7 269.9 %all-gather.11.cloned.1.call-start = ((), (), s32[]{:S(2)}) async-start(), calls=%async_computation.10 | async-start | bytes 2228224 | tf_op jit(solution)/shard_map/all_gather | solution.py:127
  11.5 354.0 %all-gather.9.cloned.1.call-start = ((), (), s32[]{:S(2)}) async-start(), calls=%async_computation.9 | async-start | bytes 2228224 | tf_op jit(solution)/shard_map/all_gather | solution.py:126
  14.1 30.2 %all-to-all-start = ((bf16[128,16,128]{0,2,1:T(8,128)(2,1)}), bf16[128,16,128]{0,2,1:T(8,128)(2,1)S(1)}, u32[]{:S(2)}, u32[]{:S(2)}) async-start(bf16[128,16,128]{0,2,1:T(8,128)(2,1)} %bitcast.19), calls=%async_computation | async-start | bytes 1048576 | tf_op jit(solution)/shard_map/all_to_all | solution.py:124
  199.5 2.9 copy-start.6
  237.6 188.2 %all-to-all-start.1 = ((bf16[128,16,256]{0,2,1:T(8,128)(2,1)}), bf16[128,16,256]{0,2,1:T(8,128)(2,1)S(1)}, u32[]{:S(2)}, u32[]{:S(2)}) async-start(bf16[128,16,256]{0,2,1:T(8,128)(2,1)} %bitcast.322), calls=%async_computation.1 | async-start | bytes 2097152 | tf_op jit(solution)/shard_map/all_to_all | solution.py:117
  244.8 414.8 %reduce-scatter.5.cloned.1.call-start = ((), (), s32[]{:S(2)}) async-start(), calls=%async_computation.8 | async-start | bytes 8912896 | tf_op jit(solution)/shard_map/reduce_scatter | solution.py:137
  368.2 48.5 %copy-start.3 = (bf16[128,2048]{1,0:T(8,128)(2,1)S(1)}, bf16[128,2048]{1,0:T(8,128)(2,1)}, u32[]{:S(2)}) copy-start(bf16[128,2048]{1,0:T(8,128)(2,1)} %param.28) | copy-start | bytes 1572868
  664.9 188.2 %copy-start.4 = (bf16[128,2048]{1,0:T(8,128)(2,1)S(1)}, bf16[128,2048]{1,0:T(8,128)(2,1)}, u32[]{:S(2)}) copy-start(bf16[128,2048]{1,0:T(8,128)(2,1)} %param.28) | copy-start | bytes 1572868
  664.9 188.2 %all-to-all-start.2 = ((bf16[16,128,2048]{2,1,0:T(8,128)(2,1)}), bf16[16,128,2048]{2,1,0:T(8,128)(2,1)}, u32[]{:S(2)}, u32[]{:S(2)}) async-start(bf16[16,128,2048]{2,1,0:T(8,128)(2,1)} %stack.2), calls=%async_computation.3 | async-start | bytes 16777216 | tf_op jit(solution)/shard_map/all_to_all | solution.py:150
  864.2 2.8 copy-start.5
  875.3 3.2 copy-start.5
  887.1 3.2 copy-start.5
  898.9 3.2 copy-start.5
  911.3 27.1 %all-to-all-start.5 = ((bf16[16,2,8192]{2,1,0:T(2,128)(2,1)}), bf16[16,2,8192]{2,1,0:T(2,128)(2,1)S(1)}, u32[]{:S(2)}, u32[]{:S(2)}) async-start(bf16[16,2,8192]{2,1,0:T(2,128)(2,1)} %reshape.421), calls=%async_computation.6 | async-start | bytes 1048576 | tf_op jit(solution)/shard_map/all_to_all | solution.py:193
  938.3 20.7 %all-to-all-start.4 = ((bf16[16,2,8192]{2,1,0:T(2,128)(2,1)}), bf16[16,2,8192]{2,1,0:T(2,128)(2,1)S(1)}, u32[]{:S(2)}, u32[]{:S(2)}) async-start(bf16[16,2,8192]{2,1,0:T(2,128)(2,1)} %reshape.419), calls=%async_computation.5 | async-start | bytes 1048576 | tf_op jit(solution)/shard_map/all_to_all | solution.py:192
  945.8 73.5 %reduce-scatter.7.cloned.1.call-start = ((), (), s32[]{:S(2)}) async-start(), calls=%async_computation.13 | async-start | bytes 557056
  950.7 15.7 %copy-start.2 = (bf16[128,2048]{1,0:T(8,128)(2,1)S(1)}, bf16[128,2048]{1,0:T(8,128)(2,1)}, u32[]{:S(2)}) copy-start(bf16[128,2048]{1,0:T(8,128)(2,1)} %reduce-scatter.5.cloned.1.call-done) | copy-start | bytes 1572868
  959.1 55.3 %all-to-all-start.3 = ((bf16[16,2,8192]{2,1,0:T(2,128)(2,1)}), bf16[16,2,8192]{2,1,0:T(2,128)(2,1)}, u32[]{:S(2)}, u32[]{:S(2)}) async-start(bf16[16,2,8192]{2,1,0:T(2,128)(2,1)} %reshape.417), calls=%async_computation.4 | async-start | bytes 1048576 | tf_op jit(solution)/shard_map/all_to_all | solution.py:191
Sparse Core Ops, SparseCore 0:
  11.0 89.5 all-gather.12
  103.7 81.3 all-gather.14
  187.7 92.9 all-gather.10
  283.1 82.2 all-gather.8
  437.8 221.8 reduce-scatter.4
  951.8 67.4 reduce-scatter.6
